TPU v7x, 32 devices: a whole 2x2x4 slice. The times are simulated.
32 devices in a mesh: rows: 8 (over z, y), sub: 4 (over x, core).
Axes of the slice: x: 2, y: 2, z: 4, core: 2. Of those that a mesh axis runs over, the one named last changes fastest.
Arguments:
- panel: float32 [12288, 256], P(('rows', 'sub'))
- trailing: float32 [12288, 1024], P(('rows', 'sub')), may hold values from -6 to 6
- live_rows: int32 [32], P(('rows', 'sub')), may hold values from 192 to 384, as said below
Outputs:
- basis: float32 [12288, 256], P(('rows', 'sub'))
- top_block: float32 [256, 1024], P(None, 'sub')
- remainder: float32 [12288, 1024], P(('rows', 'sub'))
Inputs may be any that keep to these rules, and one draw needn't show every extreme that they name: `live_rows`: the live cells of a list are its first slots; the others are padding. Some list is full and some list holds exactly 192 cells.
All inputs are finite; a program needn't handle non-finite values.
Results may differ from a plain program's by a relative error of at most 0.00014.
Values sent between devices are 32-bit elements; how exact they have to be, the bound alone decides.
No kernel may reach another device: no remote copies, remote signals or barrier semaphores. Data moves between devices by JAX's collectives and lax.ppermute only.
A program may use at most 64 MiB of HBM per device.

v0:
```python
import jax
import jax.numpy as jnp
from jax import lax
from jax.sharding import PartitionSpec as P

TILE = 128


def accumulate(left, right, tile_count):
    start_value = jnp.zeros((left.shape[1], right.shape[1]), jnp.float32)

    def add_tile(which, running):
        left_rows = lax.dynamic_slice_in_dim(left, which * TILE, TILE, 0)
        right_rows = lax.dynamic_slice_in_dim(right, which * TILE, TILE, 0)
        return running + jnp.dot(
            left_rows.T,
            right_rows,
            precision=lax.Precision.HIGHEST,
            preferred_element_type=jnp.float32,
        )

    return lax.fori_loop(0, tile_count, add_tile, start_value)


def body(panel, trailing, live_rows):
    rows_here = panel.shape[0]
    live_count = live_rows[0]
    row_index = lax.broadcasted_iota(jnp.int32, (rows_here, 1), 0)
    live_mask = row_index < live_count
    masked_panel = jnp.where(live_mask, panel, jnp.zeros_like(panel))
    masked_trail = jnp.where(live_mask, trailing, jnp.zeros_like(trailing))
    live_share = live_rows.astype(jnp.float32)
    tile_count = (live_count + TILE - 1) // TILE
    gram = accumulate(masked_panel, masked_panel, tile_count)
    gram, total = lax.psum((gram, live_share), ("rows", "sub"))
    factor = jnp.linalg.cholesky(gram / total[0])
    root_total = jnp.sqrt(total[0])
    basis = jax.scipy.linalg.solve_triangular(factor, masked_panel.T, lower=True).T
    local_top = jnp.dot(
        basis.T, masked_trail, precision=lax.Precision.HIGHEST, preferred_element_type=jnp.float32
    )
    top_whole = lax.psum(local_top, ("rows", "sub")) / root_total
    remainder = (
        masked_trail
        - jnp.dot(
            basis, top_whole, precision=lax.Precision.HIGHEST, preferred_element_type=jnp.float32
        )
        / root_total
    )
    column_width = top_whole.shape[1] // lax.axis_size("sub")
    top_block = lax.dynamic_slice_in_dim(
        top_whole, lax.axis_index("sub") * column_width, column_width, 1
    )
    return (basis, top_block, remainder)


def solution(mesh):
    in_specs = (P(("rows", "sub"), None), P(("rows", "sub"), None), P(("rows", "sub")))
    out_specs = (P(("rows", "sub"), None), P(None, "sub"), P(("rows", "sub"), None))
    return jax.shard_map(body, mesh=mesh, in_specs=in_specs, out_specs=out_specs, check_vma=False)
```

profile of v0, /device:TPU:0, one launch (start us, length us, event | category | flops | bytes accessed | tf_op | source)
XLA Modules:
  0.0 350.2 jit_solution(10997142111719962875)
XLA Ops:
  7.9 1.1 broadcast_select_fusion
  9.1 1.5 while.11
  9.1 0.5 convolution_add_fusion.2
  9.6 0.5 convolution_add_fusion.2
  10.1 0.5 convolution_add_fusion.2
  10.6 0.8 copy.6
  11.6 42.7 %psum.22 = f32[]{:T(128)} all-reduce(f32[]{:T(128)} %bitcast.1), channel_id=1, replica_groups=mesh['rows'=8,'sub'=4] {'rows','sub'}, use_global_device_ids=true, to_apply=%region_3.4 | all-reduce | flops 1 | bytes 8 | tf_op jit(solution)/shard_map/psum | solution.py:35
  54.3 87.5 %all-reduce.4.cloned.1.call-done = f32[256,256]{0,1:T(8,128)} async-done(((f32[256,256]{0,1:T(8,128)}), f32[256,256]{0,1:T(8,128)}) %all-reduce.4.cloned.1.call-update) | async-done | bytes 262160 | tf_op jit(solution)/shard_map/psum | solution.py:35
  141.8 1.7 broadcast_divide_fusion.1
  143.5 0.1 copy.7
  143.6 1.7 fusion.6
  145.3 11.7 %cholesky.49 = f32[128,128]{1,0:T(8,128)S(1)} custom-call(f32[128,128]{1,0:T(8,128)S(1)} %cholesky.115), custom_call_target="Cholesky" | custom-call | tf_op jit(solution)/shard_map/jit(cholesky)/cholesky | solution.py:36
  157.1 9.8 %custom-call.15 = f32[1,128,128]{1,2,0:T(8,128)S(1)} custom-call(f32[1,128,128]{2,1,0:T(8,128)S(1)} %get-tuple-element.59), custom_call_target="InvertDiagBlocksLowerTriangular" | custom-call | tf_op jit(solution)/shard_map/jit(cholesky)/cholesky | solution.py:36
  166.9 0.2 constant_dynamic-update-slice_fusion.1
  167.1 0.3 convolution_subtract_fusion.1
  167.4 11.7 %cholesky.103 = f32[128,128]{1,0:T(8,128)S(1)} custom-call(f32[128,128]{1,0:T(8,128)S(1)} %convolution_subtract_fusion.1), custom_call_target="Cholesky" | custom-call | tf_op jit(solution)/shard_map/jit(cholesky)/cholesky | solution.py:36
  179.2 0.6 compare_reduce_fusion
  181.2 4.0 %while.12 = (s32[]{:T(128)}, f32[256,256]{1,0:T(8,128)S(1)}, s32[2,2]{1,0:T(2,128)S(1)}, f32[2,128,128]{2,1,0:T(8,128)S(1)}, s32[]{:T(128)}) while((s32[]{:T(128)}, f32[256,256]{1,0:T(8,128)S(1)}, s32[2,2]{1,0:T(2,128)S(1)}, f32[2,128,128]{2,1,0:T(8,128)S(1)}, s32[]{:T(128)}) %tuple.44), condition=%wide.while_cond, body=%wide.while_body.sunk | while | flops 2 | bytes 131189 | solution.py:38
  181.2 0.6 fusion.27
  181.8 1.4 bitcast_dynamic-update-slice_fusion.2
  183.2 0.6 fusion.27
  183.8 1.4 bitcast_dynamic-update-slice_fusion.2
  185.2 19.9 %custom-call.16 = f32[2,128,128]{1,2,0:T(8,128)S(1)} custom-call(f32[2,128,128]{2,1,0:T(8,128)S(1)} %get-tuple-element.34), custom_call_target="InvertDiagBlocksLowerTriangular" | custom-call | tf_op jit(solution)/shard_map/jit(_solve_triangular)/triangular_solve | solution.py:38
  205.1 0.4 fusion.8
  205.5 0.5 convolution_subtract_fusion
  206.0 0.4 fusion.11
  206.4 3.0 fusion.2
  210.2 0.9 copy.8
  211.1 127.4 %all-reduce.6.cloned.1.call-done = f32[256,1024]{1,0:T(8,128)} async-done(((f32[256,1024]{1,0:T(8,128)}), f32[256,1024]{1,0:T(8,128)}) %all-reduce.6.cloned.1.call-update) | async-done | bytes 1048592 | tf_op jit(solution)/shard_map/psum | solution.py:42
  338.4 1.4 broadcast_divide_fusion
  339.9 0.7 constant_dynamic-slice_fusion.1
  340.6 2.7 divide_subtract_fusion
  (24 shorter events, 0.5 us)
Async XLA Ops:
  7.2 134.7 %all-reduce.4.cloned.1.call-start = ((), (), s32[]{:S(2)}) async-start(), calls=%async_computation | async-start | bytes 524288 | tf_op jit(solution)/shard_map/psum | solution.py:35
  9.0 2.5 copy-start.1
  11.5 327.0 %all-reduce.6.cloned.1.call-start = ((), (), s32[]{:S(2)}) async-start(), calls=%async_computation.1 | async-start | bytes 2097152 | tf_op jit(solution)/shard_map/psum | solution.py:42
  167.4 39.0 %copy-start = (f32[384,1024]{1,0:T(8,128)S(1)}, f32[384,1024]{1,0:T(8,128)}, u32[]{:S(2)}) copy-start(f32[384,1024]{1,0:T(8,128)} %param.6) | copy-start | bytes 4718596
  338.4 2.2 copy-start.2
Sparse Core Ops, SparseCore 0:
  14.1 127.7 all-reduce.3
  209.5 128.8 all-reduce.5
where the time goes:
time: 351 us; the launch traced here: 350 us
  waiting for transfers between devices  215 us (61%)
  other arithmetic  59.9 us (17%)
  blocking collectives  42.7 us (12%)
  between operations  16.9 us (5%)
  matrix products  8.9 us (3%)
  local copies, waits for them, and re-layouts  6.69 us (2%)
    psum x1, waiting for transfers between devices, body(): top_whole = lax.psum(local_top, ('rows', 'sub')) / root_total  127 us
    psum x1, waiting for transfers between devices, body(): gram, total = lax.psum((gram, live_share), ('rows', 'sub'))  87.5 us
    psum x1, blocking collectives, body(): gram, total = lax.psum((gram, live_share), ('rows', 'sub'))  42.7 us
    another operation x6, other arithmetic, body(): factor = jnp.linalg.cholesky(gram / total[0])  33.9 us
    another operation x3, other arithmetic, body(): jax.scipy.linalg.solve_triangular(factor, masked_panel.T, lower=True)  19.9 us
  transfers between devices with their start and end apart: 2, of which 2 were waited for; matrix products, arithmetic and copies ran while one was open for 0% of the time, Pallas kernels for 0%

commit v1 on v0

--- a/solution.py
+++ b/solution.py
@@ -32,7 +32,7 @@
     live_share = live_rows.astype(jnp.float32)
     tile_count = (live_count + TILE - 1) // TILE
     gram = accumulate(masked_panel, masked_panel, tile_count)
-    gram, total = lax.psum((gram, live_share), ("rows", "sub"))
+    gram, total = lax.psum(lax.psum((gram, live_share), "sub"), "rows")
     factor = jnp.linalg.cholesky(gram / total[0])
     root_total = jnp.sqrt(total[0])
     basis = jax.scipy.linalg.solve_triangular(factor, masked_panel.T, lower=True).T

time: 351 us -> 329 us (0.937)
  blocking collectives: 42.7 us -> 28.4 us
  waiting for transfers between devices: 215 us -> 208 us
    psum x1 -> x2, blocking collectives: 42.7 us -> 28.4 us  [body(): gram, total = lax.psum(lax.psum((gram, live_share), 'sub'), 'rows')]
    psum x1 -> x2, waiting for transfers between devices: 87.5 us -> 80.4 us  [body(): gram, total = lax.psum(lax.psum((gram, live_share), 'sub'), 'rows')]
  transfers between devices with their start and end apart: 2 -> 3, of which waited for: 2 -> 3; matrix products, arithmetic and copies ran while one was open for 0% -> 0% of each run, Pallas kernels for 0% -> 0%
where the time goes in v1:
time: 329 us
  waiting for transfers between devices  208 us (63%)
  other arithmetic  59.9 us (18%)
  blocking collectives  28.4 us (9%)
  between operations  16.6 us (5%)
  matrix products  8.9 us (3%)
  local copies, waits for them, and re-layouts  6.8 us (2%)
    psum x1, waiting for transfers between devices, body(): top_whole = lax.psum(local_top, ('rows', 'sub')) / root_total  128 us
    psum x2, waiting for transfers between devices, body(): gram, total = lax.psum(lax.psum((gram, live_share), 'sub'), 'rows')  80.4 us
    another operation x6, other arithmetic, body(): factor = jnp.linalg.cholesky(gram / total[0])  34 us
    psum x2, blocking collectives, body(): gram, total = lax.psum(lax.psum((gram, live_share), 'sub'), 'rows')  28.4 us
    another operation x3, other arithmetic, body(): jax.scipy.linalg.solve_triangular(factor, masked_panel.T, lower=True)  19.9 us
  transfers between devices with their start and end apart: 3, of which 3 were waited for; matrix products, arithmetic and copies ran while one was open for 0% of the time, Pallas kernels for 0%

profile of v1, /device:TPU:0, one launch (start us, length us, event | category | flops | bytes accessed | tf_op | source)
XLA Modules:
  0.0 329.0 jit_solution(4336310447908093800)
XLA Ops:
  7.9 1.1 broadcast_select_fusion
  9.1 1.5 while.11
  9.1 0.5 convolution_add_fusion.2
  9.6 0.5 convolution_add_fusion.2
  10.1 0.5 convolution_add_fusion.2
  10.6 0.8 copy.6
  11.5 34.7 %all-reduce.5.cloned.1.call-done = f32[256,256]{0,1:T(8,128)} async-done(((f32[256,256]{0,1:T(8,128)}), f32[256,256]{0,1:T(8,128)}) %all-reduce.5.cloned.1.call-update) | async-done | bytes 262160 | tf_op jit(solution)/shard_map/psum | solution.py:35
  46.3 6.3 %psum.37 = f32[1]{0:T(128)} all-reduce(f32[1]{0:T(128)S(6)} %convert_element_type.3), channel_id=1, replica_groups=mesh['rows'=8,'sub'=4] {'sub'}, use_global_device_ids=true, to_apply=%region_4.5 | all-reduce | flops 1 | bytes 8 | tf_op jit(solution)/shard_map/psum | solution.py:35
  52.6 22.1 %psum.38 = f32[]{:T(128)} all-reduce(f32[]{:T(128)} %bitcast.1), channel_id=1, replica_groups=mesh['rows'=8,'sub'=4] {'rows'}, use_global_device_ids=true, to_apply=%region_5.6 | all-reduce | flops 1 | bytes 8 | tf_op jit(solution)/shard_map/psum | solution.py:35
  74.9 45.7 %all-reduce.7.cloned.1.call-done = f32[256,256]{0,1:T(8,128)} async-done(((f32[256,256]{0,1:T(8,128)}), f32[256,256]{0,1:T(8,128)}) %all-reduce.7.cloned.1.call-update) | async-done | bytes 262160 | tf_op jit(solution)/shard_map/psum | solution.py:35
  120.5 1.6 broadcast_divide_fusion.1
  122.3 1.6 fusion.6
  124.0 11.7 %cholesky.49 = f32[128,128]{1,0:T(8,128)S(1)} custom-call(f32[128,128]{1,0:T(8,128)S(1)} %cholesky.115), custom_call_target="Cholesky" | custom-call | tf_op jit(solution)/shard_map/jit(cholesky)/cholesky | solution.py:36
  135.7 9.8 %custom-call.15 = f32[1,128,128]{1,2,0:T(8,128)S(1)} custom-call(f32[1,128,128]{2,1,0:T(8,128)S(1)} %get-tuple-element.59), custom_call_target="InvertDiagBlocksLowerTriangular" | custom-call | tf_op jit(solution)/shard_map/jit(cholesky)/cholesky | solution.py:36
  145.8 0.3 convolution_subtract_fusion.1
  146.0 11.7 %cholesky.103 = f32[128,128]{1,0:T(8,128)S(1)} custom-call(f32[128,128]{1,0:T(8,128)S(1)} %convolution_subtract_fusion.1), custom_call_target="Cholesky" | custom-call | tf_op jit(solution)/shard_map/jit(cholesky)/cholesky | solution.py:36
  157.8 0.7 compare_reduce_fusion
  159.9 4.1 %while.12 = (s32[]{:T(128)}, f32[256,256]{1,0:T(8,128)S(1)}, s32[2,2]{1,0:T(2,128)S(1)}, f32[2,128,128]{2,1,0:T(8,128)S(1)}, s32[]{:T(128)}) while((s32[]{:T(128)}, f32[256,256]{1,0:T(8,128)S(1)}, s32[2,2]{1,0:T(2,128)S(1)}, f32[2,128,128]{2,1,0:T(8,128)S(1)}, s32[]{:T(128)}) %tuple.44), condition=%wide.while_cond, body=%wide.while_body.sunk | while | flops 2 | bytes 131189 | solution.py:38
  160.0 0.6 fusion.27
  160.6 1.4 bitcast_dynamic-update-slice_fusion.2
  162.0 0.6 fusion.27
  162.6 1.4 bitcast_dynamic-update-slice_fusion.2
  164.1 19.9 %custom-call.16 = f32[2,128,128]{1,2,0:T(8,128)S(1)} custom-call(f32[2,128,128]{2,1,0:T(8,128)S(1)} %get-tuple-element.34), custom_call_target="InvertDiagBlocksLowerTriangular" | custom-call | tf_op jit(solution)/shard_map/jit(_solve_triangular)/triangular_solve | solution.py:38
  183.9 0.4 fusion.8
  184.3 0.5 convolution_subtract_fusion
  184.8 0.4 fusion.11
  185.2 3.0 fusion.2
  189.0 0.9 copy.8
  189.9 127.7 %all-reduce.9.cloned.1.call-done = f32[256,1024]{1,0:T(8,128)} async-done(((f32[256,1024]{1,0:T(8,128)}), f32[256,1024]{1,0:T(8,128)}) %all-reduce.9.cloned.1.call-update) | async-done | bytes 1048592 | tf_op jit(solution)/shard_map/psum | solution.py:42
  317.5 1.4 broadcast_divide_fusion
  319.0 0.7 constant_dynamic-slice_fusion.1
  319.7 2.7 divide_subtract_fusion
  (28 shorter events, 0.9 us)
Async XLA Ops:
  7.2 39.1 %all-reduce.5.cloned.1.call-start = ((), (), s32[]{:S(2)}) async-start(), calls=%async_computation | async-start | bytes 524288 | tf_op jit(solution)/shard_map/psum | solution.py:35
  9.0 65.7 %copy-start.1 = (f32[384,256]{1,0:T(8,128)S(1)}, f32[384,256]{1,0:T(8,128)}, u32[]{:S(2)}) copy-start(f32[384,256]{1,0:T(8,128)} %param.5) | copy-start | bytes 1179652
  11.5 109.1 %all-reduce.7.cloned.1.call-start = ((), (), s32[]{:S(2)}) async-start(), calls=%async_computation.1 | async-start | bytes 524288 | tf_op jit(solution)/shard_map/psum | solution.py:35
  46.3 271.3 %all-reduce.9.cloned.1.call-start = ((), (), s32[]{:S(2)}) async-start(), calls=%async_computation.2 | async-start | bytes 2097152 | tf_op jit(solution)/shard_map/psum | solution.py:42
  146.0 39.2 %copy-start = (f32[384,1024]{1,0:T(8,128)S(1)}, f32[384,1024]{1,0:T(8,128)}, u32[]{:S(2)}) copy-start(f32[384,1024]{1,0:T(8,128)} %param.6) | copy-start | bytes 4718596
  317.5 2.2 copy-start.2
Sparse Core Ops, SparseCore 0:
  11.6 34.6 all-reduce.4
  50.0 70.5 all-reduce.6
  188.3 129.1 all-reduce.8
